TPU v7x, 128 devices: a whole 4x4x4 slice. The times are simulated.
128 devices in a mesh: gx: 8 (over z_lo, x), gy: 4 (over z_hi, core), gz: 4 (over y).
Axes of the slice: x: 4, y: 4, z: 4 (z_hi: 2, z_lo: 2; z = z_hi * 2 + z_lo), core: 2. Of those that a mesh axis runs over, the one named last changes fastest.
Arguments:
- x_saved: bfloat16 [1024, 16384], P('gx', ('gy', 'gz')), may hold values from -0.1875 to 0.1875
- grad_out: bfloat16 [1024, 28672], P('gx', ('gz', 'gy')), may hold values from -6 to 6
- weight: bfloat16 [16384, 28672], P('gy', ('gz', 'gx')), may hold values from -0.09375 to 0.09375
Outputs:
- grad_in: bfloat16 [1024, 16384], P('gx', ('gy', 'gz'))
- grad_weight: bfloat16 [16384, 28672], P('gy', ('gz', 'gx'))
All inputs are finite; a program needn't handle non-finite values.
Results may differ from a plain program's by a relative error of at most 0.001.
Values may be sent and summed in bfloat16 or wider, within the bound.
A program may use at most 128 MiB of HBM per device.

v0:
```python
import jax
import jax.numpy as jnp
from jax import lax
from jax.sharding import PartitionSpec as P


def body(x_saved, grad_out, weight):
    token_rows = x_saved.shape[0]
    token_groups = lax.axis_size("gx")
    feature_groups = lax.axis_size("gz")
    grad_block = lax.all_gather(grad_out, "gy", axis=1, tiled=True)
    grad_all = lax.all_to_all(grad_block, "gx", split_axis=1, concat_axis=0, tiled=True)
    unit_cols = grad_all.shape[1]
    inputs_block = lax.all_gather(x_saved, "gz", axis=1, tiled=True)
    summed = jnp.einsum(
        "td,tc->dc",
        lax.all_gather(inputs_block, "gx", axis=0, tiled=True),
        grad_all,
        preferred_element_type=jnp.float32,
    )
    grad_weight = summed.astype(jnp.bfloat16)
    grad_split = grad_all.reshape(token_groups, token_rows, unit_cols)
    weight_split = weight.reshape(feature_groups, weight.shape[0] // feature_groups, unit_cols)
    terms = jnp.einsum(
        "atc,bkc->abtk", grad_split, weight_split, preferred_element_type=jnp.float32
    )
    terms = terms.reshape(token_groups * feature_groups * token_rows, weight_split.shape[1])
    grad_in = lax.psum_scatter(terms, ("gx", "gz"), scatter_dimension=0, tiled=True)
    return (grad_in.astype(jnp.bfloat16), grad_weight)


def solution(mesh):
    return jax.shard_map(
        body,
        mesh=mesh,
        in_specs=(P("gx", ("gy", "gz")), P("gx", ("gz", "gy")), P("gy", ("gz", "gx"))),
        out_specs=(P("gx", ("gy", "gz")), P("gy", ("gz", "gx"))),
        check_vma=False,
    )
```

profile of v0, /device:TPU:0, one launch (start us, length us, event | category | flops | bytes accessed | tf_op | source)
XLA Modules:
  0.0 386.5 jit_solution(9099532467425328987)
XLA Ops:
  7.2 0.0 all-gather.6.cloned.1.call-start
  7.2 0.7 all-gather.6.cloned.1.call-update
  7.9 0.0 all-gather.4.cloned.1.call-start
  7.9 2.0 copy.5
  9.9 0.0 all-gather.4.cloned.1.call-update
  10.0 0.0 all-gather.8.cloned.1.call-start
  10.0 26.1 %all-gather.6.cloned.1.call-done = bf16[128,4096]{1,0:T(8,128)(2,1)} async-done(((bf16[128,1024]{1,0:T(8,128)(2,1)}), bf16[128,4096]{1,0:T(8,128)(2,1)}) %all-gather.6.cloned.1.call-update) | async-done | bytes 1048592 | tf_op jit(solution)/shard_map/all_gather | solution.py:14
  36.1 0.0 all-gather.8.cloned.1.call-update
  36.2 0.0 reduce-scatter.2.cloned.1.call-start
  36.2 27.8 %all-gather.4.cloned.1.call-done = bf16[128,7168]{0,1:T(8,128)(2,1)} async-done(((bf16[128,1792]{0,1:T(8,128)(2,1)}), bf16[128,7168]{0,1:T(8,128)(2,1)}) %all-gather.4.cloned.1.call-update) | async-done | bytes 1835024 | tf_op jit(solution)/shard_map/all_gather | solution.py:11
  64.0 3.1 copy.6
  67.1 46.1 %all_to_all.19 = bf16[128,8,896]{2,0,1:T(8,128)(2,1)S(1)} all-to-all(bf16[128,8,896]{2,0,1:T(8,128)(2,1)S(1)} %copy.6), channel_id=1, replica_groups=mesh['gx'=8,'gy'=4,'gz'=4] {'gx'}, dimensions={1} | all-to-all | bytes 3670016 | tf_op jit(solution)/shard_map/all_to_all | solution.py:12
  113.2 0.0 copy-start
  113.2 11.8 %convolution_bitcast_fusion = f32[8,4,128,1024]{3,2,0,1:T(8,128)S(1)} fusion(bf16[4,1024,896,1]{2,1,3,0:T(8,128)(2,1)} %bitcast.22, bf16[128,8,896]{2,0,1:T(8,128)(2,1)S(1)} %all_to_all.19), kind=kOutput, calls=%fused_computation | convolution fusion | flops 7516192768 | bytes 25952256 | tf_op jit(solution)/shard_map/atc,bkc->abtk/dot_general | solution.py:24
  125.0 0.0 copy-done
  125.0 6.1 %copy.7 = f32[8,4,128,1024]{3,2,1,0:T(8,128)} copy(f32[8,4,128,1024]{3,2,0,1:T(8,128)S(1)} %convolution_bitcast_fusion) | data formatting | bytes 33554432 | tf_op jit(solution)/shard_map/atc,bkc->abtk/transpose | solution.py:24
  131.1 0.0 copy-start.1
  131.1 0.0 reduce-scatter.2.cloned.1.call-update
  131.1 43.9 %all-gather.8.cloned.1.call-done = bf16[1024,4096]{1,0:T(8,128)(2,1)} async-done(((bf16[128,4096]{1,0:T(8,128)(2,1)}), bf16[1024,4096]{1,0:T(8,128)(2,1)}) %all-gather.8.cloned.1.call-update) | async-done | bytes 8388624 | tf_op jit(solution)/shard_map/all_gather | solution.py:17
  175.0 0.0 copy-done.1
  175.1 14.2 %convolution_convert_fusion = bf16[4096,896]{1,0:T(8,128)(2,1)} fusion(bf16[1024,4096]{1,0:T(8,128)(2,1)} %all-gather.8.cloned.1.call-done, bf16[1024,896]{1,0:T(8,128)(2,1)S(1)} %bitcast.21), kind=kOutput, calls=%fused_computation.1 | convolution fusion | flops 7519862784 | bytes 17563648 | tf_op jit(solution)/shard_map/td,tc->dc/dot_general | solution.py:15
  189.3 189.0 %reduce-scatter.2.cloned.1.call-done = f32[128,1024]{1,0:T(8,128)} async-done(((f32[4096,1024]{1,0:T(8,128)}), f32[128,1024]{1,0:T(8,128)}) %reduce-scatter.2.cloned.1.call-update) | async-done | bytes 524304 | tf_op jit(solution)/shard_map/reduce_scatter | solution.py:28
  378.2 1.8 convert_element_type.6
Async XLA Ops:
  7.2 29.0 %all-gather.6.cloned.1.call-start = ((), (), s32[]{:S(2)}) async-start(), calls=%async_computation.4 | async-start | bytes 1310720 | tf_op jit(solution)/shard_map/all_gather | solution.py:14
  7.9 56.1 %all-gather.4.cloned.1.call-start = ((), (), s32[]{:S(2)}) async-start(), calls=%async_computation.2 | async-start | bytes 2293760 | tf_op jit(solution)/shard_map/all_gather | solution.py:11
  10.0 165.1 %all-gather.8.cloned.1.call-start = ((), (), s32[]{:S(2)}) async-start(), calls=%async_computation.5 | async-start | bytes 9437184 | tf_op jit(solution)/shard_map/all_gather | solution.py:17
  36.2 342.1 %reduce-scatter.2.cloned.1.call-start = ((), (), s32[]{:S(2)}) async-start(), calls=%async_computation.3 | async-start | bytes 17301504 | tf_op jit(solution)/shard_map/reduce_scatter | solution.py:28
  113.2 11.8 %copy-start = (bf16[128,8,896]{2,0,1:T(8,128)(2,1)}, bf16[128,8,896]{2,0,1:T(8,128)(2,1)S(1)}, u32[]{:S(2)}) copy-start(bf16[128,8,896]{2,0,1:T(8,128)(2,1)S(1)} %all_to_all.19) | copy-start | bytes 5505028
  131.1 43.9 %copy-start.1 = (bf16[128,8,896]{2,0,1:T(8,128)(2,1)S(1)}, bf16[128,8,896]{2,0,1:T(8,128)(2,1)}, u32[]{:S(2)}) copy-start(bf16[128,8,896]{2,0,1:T(8,128)(2,1)} %copy-done) | copy-start | bytes 5505028
Sparse Core Ops, SparseCore 0:
  9.7 26.4 all-gather.5
  38.4 25.6 all-gather.3
  65.7 109.3 all-gather.7
  177.3 200.8 reduce-scatter.1
where the time goes:
time: 387 us
  waiting for transfers between devices  288 us (74%)
  blocking collectives  46.1 us (12%)
  matrix products  26 us (7%)
  between operations  13.8 us (4%)
  local copies, waits for them, and re-layouts  11.2 us (3%)
    reduce_scatter x1, waiting for transfers between devices, body(): lax.psum_scatter(terms, ('gx', 'gz'), scatter_dimension=0, tiled=True)  189 us
    all_to_all x1, blocking collectives, body(): lax.all_to_all(grad_block, 'gx', split_axis=1, concat_axis=0, tiled=True)  46.1 us
    all_gather x1, waiting for transfers between devices, body(): lax.all_gather(inputs_block, 'gx', axis=0, tiled=True)  43.9 us
    all_gather x1, waiting for transfers between devices, body(): grad_block = lax.all_gather(grad_out, 'gy', axis=1, tiled=True)  27.8 us
    all_gather x1, waiting for transfers between devices, body(): inputs_block = lax.all_gather(x_saved, 'gz', axis=1, tiled=True)  26.1 us
    dot_general x1, matrix products, body(): jnp.einsum('td,tc->dc', lax.all_gather(inputs_block, 'gx', axis=0, tiled=...  14.2 us
    dot_general x1, matrix products, body(): jnp.einsum('atc,bkc->abtk', grad_split, weight_split, preferred_element_t...  11.8 us
  transfers between devices with their start and end apart: 4, of which 4 were waited for; matrix products, arithmetic and copies ran while one was open for 10% of the time, Pallas kernels for 0%

commit v1 on v0

--- a/solution.py
+++ b/solution.py
@@ -11,7 +11,12 @@
     grad_block = lax.all_gather(grad_out, "gy", axis=1, tiled=True)
     grad_all = lax.all_to_all(grad_block, "gx", split_axis=1, concat_axis=0, tiled=True)
     unit_cols = grad_all.shape[1]
-    inputs_block = lax.all_gather(x_saved, "gz", axis=1, tiled=True)
+    ring = [x_saved]
+    for hop in range(3):
+        ring.append(lax.ppermute(ring[-1], "gz", [(dev, (dev + 1) % 4) for dev in range(4)]))
+    inputs_block = jnp.roll(
+        jnp.concatenate(ring[::-1], axis=1), (lax.axis_index("gz") + 1) * ring[0].shape[1], axis=1
+    )
     summed = jnp.einsum(
         "td,tc->dc",
         lax.all_gather(inputs_block, "gx", axis=0, tiled=True),

time: 387 us -> 361 us (0.933)
  waiting for transfers between devices: 288 us -> 258 us
    all_gather x1, waiting for transfers between devices: 27.8 us -> 1.41 us  [body(): grad_block = lax.all_gather(grad_out, 'gy', axis=1, tiled=True)]
    all_gather x1 -> x0, waiting for transfers between devices: 26.1 us -> none  [body(): inputs_block = lax.all_gather(x_saved, 'gz', axis=1, tiled=True)]
    ppermute x0 -> x3, waiting for transfers between devices: none -> 23.8 us  [body(): lax.ppermute(ring[-1], 'gz', [(dev, (dev + 1) % 4) for dev in range(4)])]
  transfers between devices with their start and end apart: 4 -> 6, of which waited for: 4 -> 6; matrix products, arithmetic and copies ran while one was open for 10% -> 10% of each run, Pallas kernels for 0% -> 0%
where the time goes in v1:
time: 361 us
  waiting for transfers between devices  258 us (71%)
  blocking collectives  46.1 us (13%)
  matrix products  26 us (7%)
  between operations  13.8 us (4%)
  local copies, waits for them, and re-layouts  12.5 us (3%)
    reduce_scatter x1, waiting for transfers between devices, body(): lax.psum_scatter(terms, ('gx', 'gz'), scatter_dimension=0, tiled=True)  189 us
    all_to_all x1, blocking collectives, body(): lax.all_to_all(grad_block, 'gx', split_axis=1, concat_axis=0, tiled=True)  46.1 us
    all_gather x1, waiting for transfers between devices, body(): lax.all_gather(inputs_block, 'gx', axis=0, tiled=True)  43.9 us
    ppermute x3, waiting for transfers between devices, body(): lax.ppermute(ring[-1], 'gz', [(dev, (dev + 1) % 4) for dev in range(4)])  23.8 us
    dot_general x1, matrix products, body(): jnp.einsum('td,tc->dc', lax.all_gather(inputs_block, 'gx', axis=0, tiled=...  14.2 us
    dot_general x1, matrix products, body(): jnp.einsum('atc,bkc->abtk', grad_split, weight_split, preferred_element_t...  11.8 us
  transfers between devices with their start and end apart: 6, of which 6 were waited for; matrix products, arithmetic and copies ran while one was open for 10% of the time, Pallas kernels for 0%

profile of v1, /device:TPU:0, one launch (start us, length us, event | category | flops | bytes accessed | tf_op | source)
XLA Modules:
  0.0 360.7 jit_solution(5011906454834194043)
XLA Ops:
  7.2 0.0 copy-start.2
  7.2 0.0 all-gather.3.cloned.1.call-start
  7.2 2.0 copy.5
  9.2 0.0 all-gather.3.cloned.1.call-update
  9.3 0.0 all-gather.5.cloned.1.call-start
  9.3 1.7 collective-permute-start
  11.0 8.0 %collective-permute-done = bf16[128,1024]{1,0:T(8,128)(2,1)S(1)} collective-permute-done((bf16[128,1024]{1,0:T(8,128)(2,1)}, bf16[128,1024]{1,0:T(8,128)(2,1)S(1)}, u32[]{:S(2)}, u32[]{:S(2)}) %collective-permute-start) | collective-permute-done | bytes 262176 | tf_op jit(solution)/shard_map/ppermute | solution.py:16
  19.0 0.3 collective-permute-start.1
  19.3 8.3 %collective-permute-done.1 = bf16[128,1024]{1,0:T(8,128)(2,1)S(1)} collective-permute-done((bf16[128,1024]{1,0:T(8,128)(2,1)S(1)}, bf16[128,1024]{1,0:T(8,128)(2,1)S(1)}, u32[]{:S(2)}, u32[]{:S(2)}) %collective-permute-start.1) | collective-permute-done | bytes 262176 | tf_op jit(solution)/shard_map/ppermute | solution.py:16
  27.6 0.0 collective-permute-start.2
  27.6 7.6 %collective-permute-done.2 = bf16[128,1024]{1,0:T(8,128)(2,1)S(1)} collective-permute-done((bf16[128,1024]{1,0:T(8,128)(2,1)S(1)}, bf16[128,1024]{1,0:T(8,128)(2,1)S(1)}, u32[]{:S(2)}, u32[]{:S(2)}) %collective-permute-start.2) | collective-permute-done | bytes 262176 | tf_op jit(solution)/shard_map/ppermute | solution.py:16
  35.3 0.0 copy-done.2
  35.4 1.2 constant_dynamic-slice_fusion
  36.6 0.0 all-gather.5.cloned.1.call-update
  36.6 0.0 reduce-scatter.2.cloned.1.call-start
  36.7 1.4 all-gather.3.cloned.1.call-done
  38.1 3.1 copy.6
  41.1 46.1 %all_to_all.19 = bf16[128,8,896]{2,0,1:T(8,128)(2,1)S(1)} all-to-all(bf16[128,8,896]{2,0,1:T(8,128)(2,1)S(1)} %copy.6), channel_id=1, replica_groups=mesh['gx'=8,'gy'=4,'gz'=4] {'gx'}, dimensions={1} | all-to-all | bytes 3670016 | tf_op jit(solution)/shard_map/all_to_all | solution.py:12
  87.2 0.0 copy-start
  87.2 11.8 %convolution_bitcast_fusion = f32[8,4,128,1024]{3,2,0,1:T(8,128)S(1)} fusion(bf16[4,1024,896,1]{2,1,3,0:T(8,128)(2,1)} %bitcast.22, bf16[128,8,896]{2,0,1:T(8,128)(2,1)S(1)} %all_to_all.19), kind=kOutput, calls=%fused_computation | convolution fusion | flops 7516192768 | bytes 25952256 | tf_op jit(solution)/shard_map/atc,bkc->abtk/dot_general | solution.py:29
  99.0 0.0 copy-done
  99.0 6.1 %copy.7 = f32[8,4,128,1024]{3,2,1,0:T(8,128)} copy(f32[8,4,128,1024]{3,2,0,1:T(8,128)S(1)} %convolution_bitcast_fusion) | data formatting | bytes 33554432 | tf_op jit(solution)/shard_map/atc,bkc->abtk/transpose | solution.py:29
  105.1 0.0 copy-start.1
  105.1 0.0 reduce-scatter.2.cloned.1.call-update
  105.2 43.9 %all-gather.5.cloned.1.call-done = bf16[1024,4096]{1,0:T(8,128)(2,1)} async-done(((bf16[128,4096]{1,0:T(8,128)(2,1)}), bf16[1024,4096]{1,0:T(8,128)(2,1)}) %all-gather.5.cloned.1.call-update) | async-done | bytes 8388624 | tf_op jit(solution)/shard_map/all_gather | solution.py:22
  149.1 0.0 copy-done.1
  149.1 14.2 %convolution_convert_fusion = bf16[4096,896]{1,0:T(8,128)(2,1)} fusion(bf16[1024,4096]{1,0:T(8,128)(2,1)} %all-gather.5.cloned.1.call-done, bf16[1024,896]{1,0:T(8,128)(2,1)S(1)} %bitcast.21), kind=kOutput, calls=%fused_computation.1 | convolution fusion | flops 7519862784 | bytes 17563648 | tf_op jit(solution)/shard_map/td,tc->dc/dot_general | solution.py:20
  163.3 189.1 %reduce-scatter.2.cloned.1.call-done = f32[128,1024]{1,0:T(8,128)} async-done(((f32[4096,1024]{1,0:T(8,128)}), f32[128,1024]{1,0:T(8,128)}) %reduce-scatter.2.cloned.1.call-update) | async-done | bytes 524304 | tf_op jit(solution)/shard_map/reduce_scatter | solution.py:33
  352.4 1.8 convert_element_type.6
  (8 shorter events, 0.2 us)
Async XLA Ops:
  7.2 28.1 %copy-start.2 = (bf16[128,1024]{1,0:T(8,128)(2,1)S(1)}, bf16[128,1024]{1,0:T(8,128)(2,1)}, u32[]{:S(2)}) copy-start(bf16[128,1024]{1,0:T(8,128)(2,1)} %param.3) | copy-start | bytes 786436
  7.2 30.9 %all-gather.3.cloned.1.call-start = ((), (), s32[]{:S(2)}) async-start(), calls=%async_computation.2 | async-start | bytes 2293760 | tf_op jit(solution)/shard_map/all_gather | solution.py:11
  9.3 139.8 %all-gather.5.cloned.1.call-start = ((), (), s32[]{:S(2)}) async-start(), calls=%async_computation.4 | async-start | bytes 9437184 | tf_op jit(solution)/shard_map/all_gather | solution.py:22
  9.3 9.7 %collective-permute-start = (bf16[128,1024]{1,0:T(8,128)(2,1)}, bf16[128,1024]{1,0:T(8,128)(2,1)S(1)}, u32[]{:S(2)}, u32[]{:S(2)}) collective-permute-start(bf16[128,1024]{1,0:T(8,128)(2,1)} %param.3), channel_id=1, source_target_pairs={{0,1},{1,2},{2,3},{3,0},{4,5},{5,6},{6,7},{7,4},{8,9},{9,10},{10,1... | collective-permute-start | bytes 786440 | tf_op jit(solution)/shard_map/ppermute | solution.py:16
  19.0 8.6 %collective-permute-start.1 = (bf16[128,1024]{1,0:T(8,128)(2,1)S(1)}, bf16[128,1024]{1,0:T(8,128)(2,1)S(1)}, u32[]{:S(2)}, u32[]{:S(2)}) collective-permute-start(bf16[128,1024]{1,0:T(8,128)(2,1)S(1)} %collective-permute-done), channel_id=1, source_target_pairs={{0,1},{1,2},{2,3},{3,0},{4,5},{5,6},{6,7},{7,4},{8,9},{9,10},{10,1... | collective-permute-start | bytes 786440 | tf_op jit(solution)/shard_map/ppermute | solution.py:16
  27.6 7.6 %collective-permute-start.2 = (bf16[128,1024]{1,0:T(8,128)(2,1)S(1)}, bf16[128,1024]{1,0:T(8,128)(2,1)S(1)}, u32[]{:S(2)}, u32[]{:S(2)}) collective-permute-start(bf16[128,1024]{1,0:T(8,128)(2,1)S(1)} %collective-permute-done.1), channel_id=1, source_target_pairs={{0,1},{1,2},{2,3},{3,0},{4,5},{5,6},{6,7},{7,4},{8,9},{9,10},{10,1... | collective-permute-start | bytes 786440 | tf_op jit(solution)/shard_map/ppermute | solution.py:16
  36.6 315.8 %reduce-scatter.2.cloned.1.call-start = ((), (), s32[]{:S(2)}) async-start(), calls=%async_computation.3 | async-start | bytes 17301504 | tf_op jit(solution)/shard_map/reduce_scatter | solution.py:33
  87.2 11.8 %copy-start = (bf16[128,8,896]{2,0,1:T(8,128)(2,1)}, bf16[128,8,896]{2,0,1:T(8,128)(2,1)S(1)}, u32[]{:S(2)}) copy-start(bf16[128,8,896]{2,0,1:T(8,128)(2,1)S(1)} %all_to_all.19) | copy-start | bytes 5505028
  105.1 43.9 %copy-start.1 = (bf16[128,8,896]{2,0,1:T(8,128)(2,1)S(1)}, bf16[128,8,896]{2,0,1:T(8,128)(2,1)}, u32[]{:S(2)}) copy-start(bf16[128,8,896]{2,0,1:T(8,128)(2,1)} %copy-done) | copy-start | bytes 5505028
Sparse Core Ops, SparseCore 0:
  10.3 27.7 all-gather.2
  39.7 109.3 all-gather.4
  151.5 200.8 reduce-scatter.1
